TPU v7x, 512 devices: a whole 4x8x8 slice. The times are simulated.
512 devices in a mesh: band: 4 (over y_hi), row: 32 (over z, x), col: 4 (over y_lo, core).
Axes of the slice: x: 4, y: 8 (y_hi: 4, y_lo: 2; y = y_hi * 2 + y_lo), z: 8, core: 2. Of those that a mesh axis runs over, the one named last changes fastest.
Arguments:
- spectral_cube: bfloat16 [88, 128, 4096], P('band', ('row', 'col')), may hold values from -6 to 6
- aperture: int32 [128, 4096], P(('row', 'col')), may hold values 0 or 1
- measurement: float32 [128, 4444], P(('row', 'col')), may hold values from -48 to 48
- shears: int32 [88], P('band'), may hold values from 0 to 348, as said below
- step_sizes: float32 [88], P('band'), may hold values from 0.5 to 2
- spatial_weight: bfloat16 [16, 9], replicated, may hold values from -2 to 2
- spatial_bias: float32 [16], replicated, may hold values from -3 to 3
- spectral_weight: bfloat16 [7, 16, 16], replicated, may hold values from -0.5 to 0.5
- spectral_bias: float32 [16], replicated, may hold values from -3 to 3
- out_weight: float32 [16], replicated, may hold values from -1.5 to 1.5
Outputs:
- denoised: bfloat16 [88, 128, 4096], P('band', ('row', 'col'))
Inputs may be any that keep to these rules, and one draw needn't show every extreme that they name: `shears`: strictly increasing over the bands, the first 0 and the last 348.
All inputs are finite; a program needn't handle non-finite values. No bound on the sum of `aperture` on one device may be relied on, other than what follows from the above.
Results may differ from a plain program's by a relative error of at most 0.0047.
Values may be sent and summed in bfloat16 or wider, within the bound.
A program may use at most 64 MiB of HBM per device.

v0:
```python
import jax
import jax.numpy as jnp
from jax import lax
from jax.sharding import PartitionSpec as P


def with_halo(cells, sides, width):
    for axis, dim in sides:
        count = lax.axis_size(axis)
        ends = count - 1
        head = lax.slice_in_dim(cells, 0, width, axis=dim)
        tail = lax.slice_in_dim(cells, cells.shape[dim] - width, cells.shape[dim], axis=dim)
        cells = jnp.concatenate(
            [
                lax.ppermute(tail, axis, [(i, (i + 1) % count) for i in range(ends)]),
                cells,
                lax.ppermute(head, axis, [((i + 1) % count, i) for i in range(ends)]),
            ],
            axis=dim,
        )
    return cells


def denoise(
    padded,
    band_start,
    total_bands,
    block_width,
    spatial_weight,
    spatial_bias,
    spectral_weight,
    spectral_bias,
    out_weight,
):
    bands_in, rows_pad, cols_pad = padded.shape
    row_count = rows_pad - 2
    col_count = cols_pad - 2
    bands_out = bands_in - 6
    across = col_count // block_width
    band_ids = band_start + jnp.arange(bands_in, dtype=jnp.int32)
    band_valid = (band_ids >= 0) & (band_ids < total_bands)

    def one_block(block_index):
        row_index = block_index // across
        col_start = block_index % across * block_width
        window = lax.dynamic_slice(
            padded, (jnp.int32(0), row_index, col_start), (bands_in, 3, block_width + 2)
        )
        patches = jnp.stack([window[:, i, j : j + block_width] for i in range(3) for j in range(3)])
        spatial_out = (
            jnp.einsum("kq,qbc->kbc", spatial_weight, patches, preferred_element_type=jnp.float32)
            + spatial_bias[:, None, None]
        )
        active = jnp.where(band_valid[None, :, None], jax.nn.silu(spatial_out), 0.0).astype(
            jnp.bfloat16
        )
        second = (
            jnp.zeros((spatial_out.shape[0], bands_out, block_width), jnp.float32)
            + spectral_bias[:, None, None]
        )
        for d in range(spectral_weight.shape[0]):
            second = second + jnp.einsum(
                "kj,jbc->kbc",
                spectral_weight[d],
                active[:, d : d + bands_out],
                preferred_element_type=jnp.float32,
            )
        update_term = jnp.einsum(
            "k,kbc->bc", out_weight, jax.nn.silu(second), precision=lax.Precision.HIGHEST
        )
        center = window[3 : 3 + bands_out, 1, 1 : 1 + block_width].astype(jnp.float32)
        return (center + update_term).astype(jnp.bfloat16)

    blocks = lax.map(one_block, jnp.arange(row_count * across, dtype=jnp.int32))
    return (
        blocks.reshape(row_count, across, bands_out, block_width)
        .transpose(2, 0, 1, 3)
        .reshape(bands_out, row_count, col_count)
    )


def on_device(
    spectral_cube,
    aperture,
    measurement,
    shears,
    step_sizes,
    spatial_weight,
    spatial_bias,
    spectral_weight,
    spectral_bias,
    out_weight,
):
    local_bands, row_count, col_count = spectral_cube.shape
    detector_width = measurement.shape[1]
    aperture_f = aperture.astype(jnp.float32)
    masked = spectral_cube.astype(jnp.float32) * aperture_f[None]

    def place(carry, inputs):
        band_layer, offset = inputs
        empty_plane = jnp.zeros((row_count, detector_width), jnp.float32)
        placed_band = lax.dynamic_update_slice(empty_plane, band_layer, (jnp.int32(0), offset))
        opened = lax.dynamic_update_slice(empty_plane, aperture_f, (jnp.int32(0), offset))
        return ((carry[0] + placed_band, carry[1] + opened), None)

    start_sums = (
        jnp.zeros((row_count, detector_width), jnp.float32),
        jnp.zeros((row_count, detector_width), jnp.float32),
    )
    (predicted_part, count_part), _ = lax.scan(place, start_sums, (masked, shears))
    predicted, counts = lax.psum((predicted_part, count_part), "band")
    residual = (measurement - predicted) / jnp.maximum(counts, 1.0)

    def adjoint(inputs):
        offset, step_one = inputs
        pulled = lax.dynamic_slice(residual, (jnp.int32(0), offset), (row_count, col_count))
        return pulled * aperture_f * step_one

    updates = lax.map(adjoint, (shears, step_sizes))
    updated = (spectral_cube.astype(jnp.float32) + updates).astype(jnp.bfloat16)
    band_groups = lax.axis_size("band")
    total_bands = local_bands * band_groups
    col_groups = lax.axis_size("col")
    tile_width = col_count // (band_groups * col_groups)
    tiles = lax.all_to_all(
        lax.all_to_all(updated, "band", split_axis=2, concat_axis=0, tiled=True),
        "col",
        split_axis=2,
        concat_axis=1,
        tiled=True,
    )
    rimmed = with_halo(tiles, (("row", 1), (("band", "col"), 2)), 1)
    padded = jnp.pad(rimmed, ((3, 3), (0, 0), (0, 0)))
    cleaned = denoise(
        padded,
        -3,
        total_bands,
        min(tile_width, 128),
        spatial_weight,
        spatial_bias,
        spectral_weight,
        spectral_bias,
        out_weight,
    )
    returned = lax.all_to_all(
        lax.all_to_all(
            cleaned.reshape(total_bands, col_groups * row_count, 1, tile_width),
            "band",
            split_axis=0,
            concat_axis=2,
            tiled=True,
        ),
        "col",
        split_axis=1,
        concat_axis=3,
        tiled=True,
    )
    return returned.reshape(local_bands, row_count, col_count)


def solution(mesh):
    in_specs = (
        P("band", ("row", "col"), None),
        P(("row", "col"), None),
        P(("row", "col"), None),
        P("band"),
        P("band"),
        P(),
        P(),
        P(),
        P(),
        P(),
    )
    out_specs = P("band", ("row", "col"), None)
    return jax.shard_map(
        on_device, mesh=mesh, in_specs=in_specs, out_specs=out_specs, check_vma=False
    )
```

profile of v0, /device:TPU:448, one launch (start us, length us, event | category | flops | bytes accessed | tf_op | source)
XLA Modules:
  0.0 380.3 jit_solution(17812285556688412570)
XLA Ops:
  0.7 4.5 %copy.177 = bf16[22,1,4096]{0,1,2:T(2,128)(2,1)S(1)} copy(bf16[22,1,4096]{2,0,1:T(8,128)(2,1)} %param.16) | data formatting | bytes 360448 | tf_op args[0]
  5.2 12.4 %convert_multiply_fusion = f32[22,1,4096]{0,1,2:T(1,128)} fusion(bf16[22,1,4096]{0,1,2:T(2,128)(2,1)S(1)} %copy.177, f32[4096]{0:T(1024)S(1)} %bitcast.152), kind=kLoop, calls=%fused_computation.62 | loop fusion | flops 180224 | bytes 557056 | tf_op jit(solution)/shard_map/mul | solution.py:97
  17.6 4.6 %copy.178 = f32[22,1,4096]{2,1,0:T(1,128)S(1)} copy(f32[22,1,4096]{0,1,2:T(1,128)} %convert_multiply_fusion) | data formatting | bytes 720896 | tf_op jit(solution)/shard_map/while | solution.py:110
  22.2 84.4 %while.35 = (s32[]{:T(128)}, f32[1,4444]{1,0:T(1,128)S(1)}, f32[1,4444]{1,0:T(1,128)S(1)}, s32[22]{0:T(128)S(1)}, f32[22,1,4096]{2,1,0:T(1,128)S(1)}, /*index=5*...) while((s32[]{:T(128)}, f32[1,4444]{1,0:T(1,128)S(1)}, f32[1,4444]{1,0:T(1,128)S(1)}, s32[22]{0:T(128)S(1)}, ...), condition=%wide.region_1.2_spmd, body=%wide.region_0.1_spmd.sunk | while | flops 8197 | bytes 163995 | solution.py:110
  106.6 21.4 %all-reduce.1 = (f32[1,4444]{1,0:T(1,128)S(1)}, f32[1,4444]{1,0:T(1,128)S(1)}) all-reduce(f32[1,4444]{1,0:T(1,128)S(1)} %get-tuple-element.199, f32[1,4444]{1,0:T(1,128)S(1)} %get-tuple-element.198), channel_id=1, replica_groups=mesh['band'=4,'row'=32,'col'=4] {'band'}, use_global_device_ids=true, to_apply=%region_3.4 | all-reduce | flops 8888 | bytes 71104 | tf_op jit(solution)/shard_map/psum | solution.py:111
  128.1 86.3 %while.36 = (s32[]{:T(128)}, f32[22,1,4096]{2,1,0:T(1,128)S(1)}, s32[22]{0:T(128)S(1)}, f32[1,4444]{1,0:T(1,128)S(1)}, f32[1,4096]{1,0:T(1,128)S(1)}, /*index=5*/f32[22]{0:T(128)S(1)}, s32[]{:T(128)}, s32[]{:T(128)}, s32[]{:T(128)}) while((s32[]{:T(128)}, f32[22,1,4096]{2,1,0:T(1,128)S(1)}, s32[22]{0:T(128)S(1)}, f32[1,4444]{1,0:T(1,128)S(1)}, ...), condition=%wide.region_5.6_spmd, body=%wide.region_4.5_spmd.sunk | while | flops 8197 | bytes 49315 | solution.py:119
  214.4 3.6 copy.179
  218.0 5.3 %fusion.40 = bf16[4096,1,22]{2,1,0:T(2,128)(2,1)} fusion(f32[22,1,4096]{0,1,2:T(1,128)} %copy.179, bf16[22,1,4096]{0,1,2:T(2,128)(2,1)S(1)} %copy.177), kind=kLoop, calls=%fused_computation.69 | loop fusion | flops 270336 | bytes 720896
  223.8 23.4 %reduce = bf16[4096,22]{1,0:T(8,128)(2,1)S(1)} reduce(bf16[4096,1,22]{2,1,0:T(2,128)(2,1)} %fusion.40, bf16[]{:T(256)} %broadcast.25), dimensions={1}, to_apply=%fusion.40.reduce_sub_computation | reduce | bytes 360450
  247.3 2.0 reshape.32
  249.3 12.5 %all_to_all.63 = bf16[4,2,11264]{2,1,0:T(2,128)(2,1)S(1)} all-to-all(bf16[4,2,11264]{2,1,0:T(2,128)(2,1)S(1)} %reshape.32), channel_id=1, replica_groups=mesh['band'=4,'row'=32,'col'=4] {'band'}, dimensions={0} | all-to-all | bytes 360448 | tf_op jit(solution)/shard_map/all_to_all | solution.py:126
  261.8 2.6 reshape.33
  264.4 2.3 copy.180
  267.4 2.3 reduce.1
  270.2 7.5 %all_to_all.64 = bf16[4,2,11264]{2,1,0:T(2,128)(2,1)S(1)} all-to-all(bf16[4,2,11264]{2,1,0:T(2,128)(2,1)S(1)} %reshape.34), channel_id=1, replica_groups=mesh['band'=4,'row'=32,'col'=4] {'col'}, dimensions={0} | all-to-all | bytes 360448 | tf_op jit(solution)/shard_map/all_to_all | solution.py:125
  277.6 1.0 reshape.35
  279.3 3.4 collective-permute-start
  282.8 4.7 %collective-permute-start.1 = (bf16[88,1,256]{2,1,0:T(2,128)(2,1)S(1)}, bf16[88,1,256]{2,1,0:T(2,128)(2,1)S(1)}, u32[]{:S(2)}, u32[]{:S(2)}) collective-permute-start(bf16[88,1,256]{2,1,0:T(2,128)(2,1)S(1)} %get-tuple-element.391), channel_id=1, source_target_pairs={{4,0},{8,4},{12,8},{16,12},{20,16},{24,20},{28,24},{32,28},{36,32}... | collective-permute-start | bytes 135176 | tf_op jit(solution)/shard_map/ppermute | solution.py:17
  287.8 1.7 collective-permute-done.1
  290.0 1.3 collective-permute-start.2
  291.3 1.3 collective-permute-start.3
  292.6 2.6 collective-permute-done.3
  295.2 0.9 pad_maximum_fusion
  296.4 58.9 %while.37 = (s32[]{:T(128)}, bf16[8,88,128]{2,1,0:T(8,128)(2,1)S(1)}, s32[8]{0:T(128)S(1)}, bf16[94,6,258]{2,0,1:T(8,128)(2,1)S(1)}, f32[16]{0:T(128)S(1)}, /*in...) while((s32[]{:T(128)}, ...), condition=%wide.region_7.8_spmd.clone, body=%wide.region_6.7_spmd.clone.sunk | while | flops 49362328 | bytes 14682244 | solution.py:74
  300.2 0.8 stack.8
  307.6 0.8 stack.8
  314.9 0.8 stack.8
  329.6 0.8 stack.8
  337.0 0.8 stack.8
  344.3 0.8 stack.8
  355.6 16.2 %all_to_all.65 = bf16[88,4,1,256]{3,1,2,0:T(4,128)(2,1)S(1)} all-to-all(bf16[88,4,1,256]{3,1,2,0:T(4,128)(2,1)S(1)} %copy.186), channel_id=1, replica_groups=mesh['band'=4,'row'=32,'col'=4] {'band'}, dimensions={0} | all-to-all | bytes 360448 | tf_op jit(solution)/shard_map/all_to_all | solution.py:146
  371.9 7.5 %all_to_all.66 = bf16[22,4,4,256]{3,2,0,1:T(4,128)(2,1)S(1)} all-to-all(bf16[22,4,4,256]{3,2,0,1:T(4,128)(2,1)S(1)} %copy.187), channel_id=1, replica_groups=mesh['band'=4,'row'=32,'col'=4] {'col'}, dimensions={1} | all-to-all | bytes 360448 | tf_op jit(solution)/shard_map/all_to_all | solution.py:145
  (376 shorter events, 125.0 us)
Async XLA Ops:
  17.6 4.6 %copy-start.4 = (s32[22]{0:T(128)S(1)}, s32[22]{0:T(128)}, u32[]{:S(2)}) copy-start(s32[22]{0:T(128)} %param.19) | copy-start | bytes 268
  17.6 110.4 %copy-start.1 = (f32[1,4444]{1,0:T(1,128)S(1)}, f32[1,4444]{1,0:T(1,128)}, u32[]{:S(2)}) copy-start(f32[1,4444]{1,0:T(1,128)} %param.18) | copy-start | bytes 53332
  17.6 110.5 %copy-start.5 = (f32[22]{0:T(128)S(1)}, f32[22]{0:T(128)}, u32[]{:S(2)}) copy-start(f32[22]{0:T(128)} %param.20) | copy-start | bytes 268
  279.3 8.5 %collective-permute-start = (bf16[88,1,256]{2,1,0:T(2,128)(2,1)S(1)}, bf16[88,1,256]{2,1,0:T(2,128)(2,1)S(1)}, u32[]{:S(2)}, u32[]{:S(2)}) collective-permute-start(bf16[88,1,256]{2,1,0:T(2,128)(2,1)S(1)} %get-tuple-element.390), channel_id=1, source_target_pairs={{0,4},{4,8},{8,12},{12,16},{16,20},{20,24},{24,28},{28,32},{32,36}... | collective-permute-start | bytes 135176 | tf_op jit(solution)/shard_map/ppermute | solution.py:15
  282.7 13.7 %copy-start = (bf16[7,16,16]{2,1,0:T(8,128)(2,1)S(1)}, bf16[7,16,16]{2,1,0:T(8,128)(2,1)}, u32[]{:S(2)}) copy-start(bf16[7,16,16]{2,1,0:T(8,128)(2,1)} %param.23) | copy-start | bytes 10756
  282.7 13.7 %copy-start.2 = (f32[16]{0:T(128)S(1)}, f32[16]{0:T(128)}, u32[]{:S(2)}) copy-start(f32[16]{0:T(128)} %param.24) | copy-start | bytes 196
  282.7 13.7 %copy-start.3 = (bf16[16,9]{1,0:T(8,128)(2,1)S(1)}, bf16[16,9]{1,0:T(8,128)(2,1)}, u32[]{:S(2)}) copy-start(bf16[16,9]{1,0:T(8,128)(2,1)} %param.21) | copy-start | bytes 868
  282.7 13.7 %copy-start.6 = (f32[16]{0:T(128)S(1)}, f32[16]{0:T(128)}, u32[]{:S(2)}) copy-start(f32[16]{0:T(128)} %param.22) | copy-start | bytes 196
  282.8 13.7 %copy-start.7 = (f32[16]{0:T(128)S(1)}, f32[16]{0:T(128)}, u32[]{:S(2)}) copy-start(f32[16]{0:T(128)} %param.25) | copy-start | bytes 196
  282.8 6.8 %collective-permute-start.1 = (bf16[88,1,256]{2,1,0:T(2,128)(2,1)S(1)}, bf16[88,1,256]{2,1,0:T(2,128)(2,1)S(1)}, u32[]{:S(2)}, u32[]{:S(2)}) collective-permute-start(bf16[88,1,256]{2,1,0:T(2,128)(2,1)S(1)} %get-tuple-element.391), channel_id=1, source_target_pairs={{4,0},{8,4},{12,8},{16,12},{20,16},{24,20},{28,24},{32,28},{36,32}... | collective-permute-start | bytes 135176 | tf_op jit(solution)/shard_map/ppermute | solution.py:17
  290.0 2.6 collective-permute-start.2
  291.3 3.9 %collective-permute-start.3 = (bf16[88,6,1]{2,1,0:T(8,128)(2,1)S(1)}, bf16[88,6,1]{2,1,0:T(8,128)(2,1)S(1)}, u32[]{:S(2)}, u32[]{:S(2)}) collective-permute-start(bf16[88,6,1]{2,1,0:T(8,128)(2,1)S(1)} %get-tuple-element.389), channel_id=1, source_target_pairs={{1,0},{2,1},{3,2},{128,3},{129,128},{130,129},{131,130},{256,131},... | collective-permute-start | bytes 3176 | tf_op jit(solution)/shard_map/ppermute | solution.py:17
where the time goes:
time: 388 us; the launch traced here: 380 us
  local copies, waits for them, and re-layouts  108 us (28%)
  loops' own time  105 us (27%)
  other arithmetic  65.6 us (17%)
  blocking collectives  65.1 us (17%)
  matrix products  20.6 us (5%)
  starting transfers between devices  10.7 us (3%)
  waiting for transfers between devices  4.72 us (1%)
    another operation x1, loops' own time, on_device(): lax.scan(place, start_sums, (masked, shears))  41.9 us
    another operation x1, loops' own time, on_device(): updates = lax.map(adjoint, (shears, step_sizes))  41.5 us
    unnamed x3, other arithmetic  31 us
    dynamic_slice x44, local copies, waits for them, and re-layouts, on_device(): lax.scan(place, start_sums, (masked, shears))  28.6 us
    add x44, local copies, waits for them, and re-layouts, place(): return ((carry[0] + placed_band, carry[1] + opened), None)  25.1 us
    another operation x1, loops' own time, denoise(): blocks = lax.map(one_block, jnp.arange(row_count * across, dtype=jnp.int32))  21.6 us
    psum x1, blocking collectives, on_device(): predicted, counts = lax.psum((predicted_part, count_part), 'band')  21.4 us
    all_to_all x1, blocking collectives, on_device(): lax.all_to_all(cleaned.reshape(total_bands, col_groups * row_count, 1, ti...  16.2 us
  transfers between devices with their start and end apart: 4, of which 3 were waited for; matrix products, arithmetic and copies ran while one was open for 0% of the time, Pallas kernels for 0%

commit v1 on v0

v1 whole, which is shorter than its diff:
```python
import jax
import jax.numpy as jnp
from jax import lax
from jax.experimental import pallas as pl
from jax.experimental.pallas import tpu as pltpu
from jax.sharding import PartitionSpec as P

MESH = pl.DeviceIdType.MESH
F32 = jnp.float32
BF16 = jnp.bfloat16
LANES = 128
BANDS = 22
HALO = 3
CH = 16
SLOTS = 28
ACT = SLOTS * CH
TILE = 256


def iota(shape, dim):
    return lax.broadcasted_iota(jnp.int32, shape, dim)


def column_of(row, rows, where):
    shape = (rows, row.shape[1])
    return jnp.sum(
        jnp.where(where(iota(shape, 0), iota(shape, 1)), row, 0.0), axis=1, keepdims=True
    )


def pieces(x):
    high = x.astype(BF16).astype(F32)
    middle = (x - high).astype(BF16).astype(F32)
    return high, middle, x - high - middle


def gather_lanes(x, index):
    return jnp.take_along_axis(x, index, axis=1, mode="promise_in_bounds")


def project(cube, aperture, shears, part):
    rows = 24
    tiles = cube.shape[1] // LANES
    shift = column_of(shears[...].astype(F32), rows, lambda i, l: i == l).astype(jnp.int32)
    lane = iota((rows, LANES), 1)
    within = jnp.broadcast_to(shift & (LANES - 1), (rows, LANES))
    index = (lane - within) & (LANES - 1)
    steps = (shift >> 7) + jnp.where(lane < within, 1, 0)
    own = iota((rows, LANES), 0) < BANDS
    masked, opened = [], []
    none = jnp.zeros((rows, LANES), F32)
    for t in range(part.shape[1] // LANES):
        if t < tiles:
            at = slice(t * LANES, (t + 1) * LANES)
            open_t = aperture[:, at].astype(F32)
            band_t = jnp.concatenate([cube[:, at].astype(F32), jnp.zeros((rows - BANDS, LANES), F32)])
            masked.append(gather_lanes(band_t * open_t, index))
            opened.append(gather_lanes(jnp.where(own, open_t, 0.0), index))
        else:
            masked.append(none)
            opened.append(none)
        for row, placed in enumerate((masked, opened)):
            back = [placed[t - e] if t >= e else none for e in range(4)]
            here = jnp.where(
                steps == 0, back[0], jnp.where(steps == 1, back[1], jnp.where(steps == 2, back[2], back[3]))
            )
            part[row : row + 1, t * LANES : (t + 1) * LANES] = jnp.sum(
                here, axis=0, keepdims=True
            ).astype(part.dtype)


def pack_small(shears, steps, small):
    small[...] = jnp.zeros_like(small)
    small[0:1, 0:BANDS] = shears[...].astype(F32)
    small[1:2, 0:BANDS] = steps[...]


def pack_edges(cube, low, high):
    for t in range(0, cube.shape[1], 512):
        at = slice(t, t + 512)
        bands = cube[:, at].astype(F32)
        none = jnp.zeros((1, 512), F32)
        low[:, at] = jnp.concatenate([bands[0:HALO], none]).astype(BF16)
        high[:, at] = jnp.concatenate([bands[BANDS - HALO :], none]).astype(BF16)


def expand_spatial(weight, bias, band, groups, one, two):
    half = 0.5 * column_of(bias[...], CH, lambda i, l: i == l)
    parts = pieces(half)
    taps = weight.shape[1]
    depth = (taps + 1) * CH
    spread = (iota((taps, depth), 1) // CH == iota((taps, depth), 0)).astype(BF16)
    wide = jnp.dot(weight[...] * jnp.bfloat16(0.5), spread, preferred_element_type=F32)
    col = iota((CH, depth), 1)
    bias_row = jnp.where(
        col == taps * CH,
        parts[0],
        jnp.where(col == taps * CH + 1, parts[1], jnp.where(col == taps * CH + 2, parts[2], 0.0)),
    )
    in_taps = col < taps * CH
    slot = col & (CH - 1)

    def block(wanted):
        return jnp.where(in_taps, jnp.where(slot == wanted, wide, 0.0), bias_row)

    for b in range(CH):
        one[b * CH : (b + 1) * CH, :] = block(b).astype(BF16)
    slots = [0, 1, 2, 3, 4, 5, 8, 9, 10, 12, 13, 14]
    for n, s in enumerate(slots):
        value = block(s)
        if 8 <= s < 12:
            value = jnp.where(band > 0, value, 0.0)
        if s >= 12:
            value = jnp.where(band < groups - 1, value, 0.0)
        two[n * CH : (n + 1) * CH, :] = value.astype(BF16)


def expand_spectral(weight, bias, out):
    depth = out.shape[1]
    rows = 24
    half = 0.5 * column_of(bias[...], CH, lambda i, l: i == l)
    parts = pieces(half)
    spread = ((iota((CH, depth), 1) & (CH - 1)) == iota((CH, depth), 0)).astype(BF16)
    wide = jnp.dot(weight[...] * jnp.bfloat16(0.5), spread, preferred_element_type=F32)
    col = iota((rows, depth), 1)
    slot = col >> 4
    place = jnp.where(slot < BANDS, slot + HALO, jnp.where(slot < BANDS + HALO, slot - BANDS, slot))
    band = iota((rows, depth), 0)
    tap = jnp.where((slot < SLOTS) & (band < BANDS), place - band, -1)
    taps = weight.shape[0] // CH
    for k in range(CH):
        block = jnp.where(col == ACT, parts[0][k : k + 1], 0.0)
        block = jnp.where(col == ACT + 1, parts[1][k : k + 1], block)
        block = jnp.where(col == ACT + 2, parts[2][k : k + 1], block)
        for d in range(taps):
            block = jnp.where(tap == d, wide[d * CH + k : d * CH + k + 1], block)
        out[k * rows : (k + 1) * rows, :] = block.astype(BF16)


def refresh(cubes, apertures, lows, highs, residuals, smalls, row, rows, upd):
    width = cubes[0].shape[1]
    own, below, above = (s[...] for s in smalls)

    def column(n):
        return (
            column_of(own[n : n + 1], 32, lambda i, l: (i == l) & (i < BANDS))
            + column_of(below[n : n + 1], 32, lambda i, l: (i - 24 + BANDS - HALO == l) & (i >= 24) & (i < 24 + HALO))
            + column_of(above[n : n + 1], 32, lambda i, l: (i - 28 == l) & (i >= 28) & (i < 28 + HALO))
        )

    shift = column(0).astype(jnp.int32)
    step = jnp.broadcast_to(column(1), (32, LANES))
    lane = iota((32, LANES), 1)
    within = jnp.broadcast_to(shift & (LANES - 1), (32, LANES))
    index = (lane + within) & (LANES - 1)
    steps = (shift >> 7) + jnp.where(lane + within >= LANES, 1, 0)
    is0, is1, is2 = steps == 0, steps == 1, steps == 2
    margin = jnp.zeros((32, LANES), BF16)
    for i in range(3):
        upd[i, :, 0:LANES] = margin
        upd[i, :, LANES + width : 2 * LANES + width] = margin
        inside = (row + i >= 1) & (row + i <= rows)

        def pull(t, i=i):
            at = pl.ds(pl.multiple_of(t * LANES, LANES), LANES)
            return gather_lanes(jnp.broadcast_to(residuals[i][:, at], (32, LANES)), index)

        def tile(t, carry, i=i, inside=inside):
            p0, p1, p2 = carry
            p3 = pull(t + 3)
            at = pl.ds(pl.multiple_of(t * LANES, LANES), LANES)
            pulled = jnp.where(is0, p0, jnp.where(is1, p1, jnp.where(is2, p2, p3)))
            cube = jnp.concatenate(
                [
                    cubes[i][:, at].astype(F32),
                    jnp.zeros((2, LANES), F32),
                    lows[i][:, at].astype(F32),
                    highs[i][:, at].astype(F32),
                ]
            )
            new = cube + pulled * apertures[i][:, at].astype(F32) * step
            new = jnp.where(inside, new, 0.0)
            upd[i, :, pl.ds(pl.multiple_of(t * LANES + LANES, LANES), LANES)] = new.astype(BF16)
            return p1, p2, p3

        lax.fori_loop(0, width // LANES, tile, (pull(0), pull(1), pull(2)))


def denoise(upd, one, two, spectral, out_weight, active, out):
    width = out.shape[1]
    ones = jnp.ones((CH, TILE), BF16)
    active[ACT:, :] = ones
    project_out = column_of(out_weight[...], CH, lambda i, l: i == l)

    def tile(t, carry):
        start = pl.multiple_of(t * TILE, TILE)
        window = [upd[i, :, pl.ds(start, TILE + 2 * LANES)] for i in range(3)]
        shifted = [window[i][:, LANES - 1 + j : LANES - 1 + j + TILE] for i in range(3) for j in range(3)]
        for weight, group, at in ((one, slice(0, 16), 0), (two, slice(16, 32), 16 * CH)):
            patch = jnp.concatenate([s[group] for s in shifted] + [ones])
            half = jnp.dot(weight[...], patch, preferred_element_type=F32)
            active[at : at + half.shape[0], :] = (half * jnp.tanh(half) + half).astype(BF16)
        half = jnp.dot(spectral[...], active[...], preferred_element_type=F32)
        total = shifted[4].astype(F32)[0:24]
        for k in range(CH):
            h = half[k * 24 : (k + 1) * 24]
            total = total + project_out[k : k + 1] * (h * jnp.tanh(h) + h)
        out[:, pl.ds(start, TILE)] = total[0:BANDS].astype(BF16)
        return carry

    lax.fori_loop(0, width // TILE, tile, 0)


def prepare_kernel(groups, cube, aperture, shears, steps, sw, sb, pw, pb, part, low, high, small, one, two, spectral):
    project(cube, aperture, shears, part)
    pack_small(shears, steps, small)
    pack_edges(cube, low, high)
    expand_spatial(sw, sb, lax.axis_index("band"), groups, one, two)
    expand_spectral(pw, pb, spectral)


def exchange_kernel(
    sizes,
    cube, aperture, meas, part, low, high, small,
    cube_up, cube_down, ap_up, ap_down, lows, highs, small_low, small_high, res, res_up, res_down,
    parts, send, recv, barrier_dummy=None,
):
    groups, nrow, ncol = sizes
    band, row, col = lax.axis_index("band"), lax.axis_index("row"), lax.axis_index("col")
    count = nrow * ncol
    flat = row * ncol + col

    def device(db, dr):
        r = lax.rem(flat + dr + count, count)
        return (lax.rem(band + db + groups, groups), r // ncol, lax.rem(r, ncol))

    peers = [(db, dr) for db in (-1, 1) for dr in (-1, 0, 1)] + [(2, 0), (0, -1), (0, 1)]
    barrier = pltpu.get_barrier_semaphore()
    for peer in peers:
        pl.semaphore_signal(barrier, inc=1, device_id=device(*peer), device_id_type=MESH)
    pl.semaphore_wait(barrier, len(peers))

    used = [0]

    def copy(src, dst, peer):
        n = used[0]
        used[0] += 1
        return pltpu.make_async_remote_copy(
            src_ref=src, dst_ref=dst, send_sem=send.at[n], recv_sem=recv.at[n],
            device_id=device(*peer), device_id_type=MESH,
        )

    partial = [copy(part, parts.at[n], (db, 0)) for n, db in enumerate((1, 2, -1))]
    bulk = [
        copy(small, small_low, (1, 0)),
        copy(small, small_high, (-1, 0)),
        copy(aperture, ap_up, (0, 1)),
        copy(aperture, ap_down, (0, -1)),
    ]
    for dr in (0, 1, -1):
        bulk.append(copy(high, lows.at[1 - dr], (1, dr)))
        bulk.append(copy(low, highs.at[1 - dr], (-1, dr)))
    bulk += [copy(cube, cube_up, (0, 1)), copy(cube, cube_down, (0, -1))]
    last = [copy(res, res_up, (0, 1)), copy(res, res_down, (0, -1))]
    for c in partial + bulk:
        c.start()
    for c in partial:
        c.wait_recv()
    width = meas.shape[1]
    total = part[...].astype(F32) + (parts[0].astype(F32) + parts[1].astype(F32) + parts[2].astype(F32))
    predicted, counts = total[0:1, 0:width], total[1:2, 0:width]
    res[:, 4352:] = jnp.zeros((1, res.shape[1] - 4352), F32)
    res[:, 0:width] = (meas[...] - predicted) / jnp.maximum(counts, 1.0)
    for c in last:
        c.start()
    for c in bulk + last:
        c.wait_recv()
    for c in partial + bulk + last:
        c.wait_send()


def finish_kernel(sizes, *refs):
    (cube, cube_up, cube_down, ap, ap_up, ap_down, lows, highs, small, small_low, small_high,
     res, res_up, res_down, one, two, spectral, out_weight, out, upd, active) = refs
    groups, nrow, ncol = sizes
    flat = lax.axis_index("row") * ncol + lax.axis_index("col")
    refresh(
        (cube_up, cube, cube_down),
        (ap_up, ap, ap_down),
        [lows.at[i] for i in range(3)],
        [highs.at[i] for i in range(3)],
        (res_up, res, res_down),
        (small, small_low, small_high),
        flat,
        nrow * ncol,
        upd,
    )
    denoise(upd, one, two, spectral, out_weight, active, out)


def solution(mesh):
    sizes = tuple(mesh.shape[a] for a in ("band", "row", "col"))
    vmem = pl.BlockSpec(memory_space=pltpu.VMEM)

    def on_device(cube, aperture, meas, shears, steps, sw, sb, pw, pb, ow):
        width = cube.shape[2]
        cube = cube.reshape(cube.shape[0], width)
        shears, steps, sb, pb, ow = (a.reshape(1, -1) for a in (shears, steps, sb, pb, ow))
        pw = pw.reshape(-1, CH)
        wide = (meas.shape[1] + 2 * LANES - 1) // LANES * LANES
        shape = jax.ShapeDtypeStruct
        edge = shape((4, width), BF16)
        part, low, high, small, one, two, spectral = pl.pallas_call(
            lambda *r: prepare_kernel(sizes[0], *r),
            name="prepare",
            out_shape=(
                shape((2, wide), F32), edge, edge, shape((8, LANES), F32),
                shape((16 * CH, 10 * CH), BF16), shape((12 * CH, 10 * CH), BF16), shape((24 * CH, ACT + CH), BF16),
            ),
            in_specs=[vmem] * 8,
            out_specs=(vmem,) * 7,
        )(cube, aperture, shears, steps, sw, sb, pw, pb)
        row = shape((1, wide), F32)
        halos = pl.pallas_call(
            lambda *r: exchange_kernel(sizes, *r),
            name="exchange",
            out_shape=(
                shape(cube.shape, BF16), shape(cube.shape, BF16), shape(aperture.shape, jnp.int32), shape(aperture.shape, jnp.int32),
                shape((3, 4, width), BF16), shape((3, 4, width), BF16), shape((8, LANES), F32), shape((8, LANES), F32), row, row, row,
            ),
            in_specs=[vmem] * 7,
            out_specs=(vmem,) * 11,
            scratch_shapes=[
                pltpu.VMEM((3, 2, wide), F32),
                pltpu.SemaphoreType.DMA((17,)),
                pltpu.SemaphoreType.DMA((17,)),
            ],
            compiler_params=pltpu.CompilerParams(collective_id=0, has_side_effects=True),
        )(cube, aperture, meas, part, low, high, small)
        cube_up, cube_down, ap_up, ap_down, lows, highs, small_low, small_high, res, res_up, res_down = halos
        out = pl.pallas_call(
            lambda *r: finish_kernel(sizes, *r),
            name="finish",
            out_shape=shape(cube.shape, BF16),
            in_specs=[vmem] * 18,
            out_specs=vmem,
            scratch_shapes=[
                pltpu.VMEM((3, 32, width + 2 * LANES), BF16),
                pltpu.VMEM((ACT + CH, TILE), BF16),
            ],
        )(cube, cube_up, cube_down, aperture, ap_up, ap_down, lows, highs, small, small_low, small_high,
          res, res_up, res_down, one, two, spectral, ow)
        return out.reshape(out.shape[0], 1, width)

    in_specs = (
        P("band", ("row", "col"), None),
        P(("row", "col"), None),
        P(("row", "col"), None),
        P("band"),
        P("band"),
        P(),
        P(),
        P(),
        P(),
        P(),
    )
    return jax.shard_map(
        on_device, mesh=mesh, in_specs=in_specs, out_specs=P("band", ("row", "col"), None), check_vma=False
    )
```

time: 388 us -> 54.4 us (0.14)
  the two profiles are of different devices: /device:TPU:448 before, /device:TPU:16 now
where the time goes in v1:
time: 54.4 us; the launch traced here: 54.2 us
  Pallas kernels  54.2 us (100%)
    pallas_call x1, Pallas kernels, on_device(): pl.pallas_call(lambda *r: exchange_kernel(sizes, *r), name='exchange', ou...  31.2 us
    pallas_call x1, Pallas kernels, on_device(): pl.pallas_call(lambda *r: finish_kernel(sizes, *r), name='finish', out_sh...  20.3 us
    pallas_call x1, Pallas kernels, on_device(): pl.pallas_call(lambda *r: prepare_kernel(sizes[0], *r), name='prepare', o...  2.65 us

profile of v1, /device:TPU:16, one launch (start us, length us, event | category | flops | bytes accessed | tf_op | source)
XLA Modules:
  0.0 54.2 jit_solution(9828533419672265618)
XLA Ops:
  0.0 2.6 %prepare.1 = (f32[2,4608]{1,0:T(2,128)}, bf16[4,4096]{1,0:T(4,128)(2,1)}, bf16[4,4096]{1,0:T(4,128)(2,1)}, f32[8,128]{1,0:T(8,128)}, bf16[256,160]{1,0:T(8,128)(...) custom-call(bf16[22,4096]{1,0:T(8,128)(2,1)} %bitcast.8, s32[1,4096]{1,0:T(1,128)} %r_3_.1, s32[1,22]{1,0:T(1,128)} %bitcast.13, ...), custom_call_target="tpu_custom_call" | custom-call | tf_op jit(solution)/shard_map/prepare/pallas_call | solution.py:313
  2.6 31.2 %exchange.1 = (bf16[22,4096]{1,0:T(8,128)(2,1)}, bf16[22,4096]{1,0:T(8,128)(2,1)}, s32[1,4096]{1,0:T(1,128)}, s32[1,4096]{1,0:T(1,128)}, bf16[3,4,4096]{2,1,0:T(...) custom-call(bf16[22,4096]{1,0:T(8,128)(2,1)} %bitcast.9, ...), custom_call_target="tpu_custom_call" | custom-call | tf_op jit(solution)/shard_map/exchange/pallas_call | solution.py:324
  33.8 20.3 %finish.1 = bf16[22,4096]{1,0:T(8,128)(2,1)} custom-call(bf16[22,4096]{1,0:T(8,128)(2,1)} %bitcast.10, bf16[22,4096]{1,0:T(8,128)(2,1)} %get-tuple-element.27.r_1_, bf16[22,4096]{1,0:T(8,128)(2,1)} %get-tuple-element.28.r_2_, s32[1,4096]{1,0:T(1,128)} %r_3_.1, s32[1,4096]{1,0:T(1,128)} %get-tuple-element.29.r_4_, s32[1,4096]{1,0:T(1,128)} %get-tuple-element.30.r_5_, ...), custom_call_target="tpu_custom_call" | custom-call | tf_op jit(solution)/shard_map/finish/pallas_call | solution.py:341

commit v2 on v1

v2 whole, which is shorter than its diff:
```python
import jax
import jax.numpy as jnp
from jax import lax
from jax.experimental import pallas as pl
from jax.experimental.pallas import tpu as pltpu
from jax.sharding import PartitionSpec as P

MESH = pl.DeviceIdType.MESH
F32 = jnp.float32
BF16 = jnp.bfloat16
LANES = 128
BANDS = 22
HALO = 3
CH = 16
SLOTS = 28
ACT = SLOTS * CH
TILE = 256


def iota(shape, dim):
    return lax.broadcasted_iota(jnp.int32, shape, dim)


def column_of(row, rows, where):
    shape = (rows, row.shape[1])
    return jnp.sum(
        jnp.where(where(iota(shape, 0), iota(shape, 1)), row, 0.0), axis=1, keepdims=True
    )


def pieces(x):
    high = x.astype(BF16).astype(F32)
    middle = (x - high).astype(BF16).astype(F32)
    return high, middle, x - high - middle


def gather_lanes(x, index):
    return jnp.take_along_axis(x, index, axis=1, mode="promise_in_bounds")


def place(tiles, shift, out, tile_of):
    rows = shift.shape[0]
    lane = iota((rows, LANES), 1)
    within = jnp.broadcast_to(shift & (LANES - 1), (rows, LANES))
    index = (lane - within) & (LANES - 1)
    steps = (shift >> 7) + jnp.where(lane < within, 1, 0)
    is0, is1, is2 = steps == 0, steps == 1, steps == 2
    none = jnp.zeros((rows, LANES), F32)
    turned = []
    for t in range(out.shape[1] // LANES):
        turned.append(gather_lanes(tile_of(t), index) if t < tiles else none)
        back = [turned[t - e] if t >= e else none for e in range(4)]
        here = jnp.where(is0, back[0], jnp.where(is1, back[1], jnp.where(is2, back[2], back[3])))
        out[:, t * LANES : (t + 1) * LANES] = jnp.sum(here, axis=0, keepdims=True)


def shift_column(row):
    return column_of(row, 24, lambda i, l: i == l).astype(jnp.int32)


def project(cube, aperture, shears, part):
    def masked(t):
        at = slice(t * LANES, (t + 1) * LANES)
        bands = jnp.concatenate([cube[:, at].astype(F32), jnp.zeros((24 - BANDS, LANES), F32)])
        return bands * aperture[:, at].astype(F32)

    place(cube.shape[1] // LANES, shift_column(shears[...].astype(F32)), part, masked)


def count_open(aperture, smalls, out):
    shift = jnp.concatenate([shift_column(s[0:1]) for s in smalls])
    shape = (shift.shape[0], LANES)
    group_row = jnp.concatenate([iota((24, LANES), 0)] * len(smalls))
    own = group_row < BANDS

    def opened(t):
        open_t = aperture[:, t * LANES : (t + 1) * LANES].astype(F32)
        return jnp.where(own, jnp.broadcast_to(open_t, shape), 0.0)

    place(aperture.shape[1] // LANES, shift, out, opened)


def pack_small(shears, steps, small):
    small[...] = jnp.zeros_like(small)
    small[0:1, 0:BANDS] = shears[...].astype(F32)
    small[1:2, 0:BANDS] = steps[...]


def pack_edges(cube, low, high):
    for t in range(0, cube.shape[1], 512):
        at = slice(t, t + 512)
        bands = cube[:, at].astype(F32)
        none = jnp.zeros((1, 512), F32)
        low[:, at] = jnp.concatenate([bands[0:HALO], none]).astype(BF16)
        high[:, at] = jnp.concatenate([bands[BANDS - HALO :], none]).astype(BF16)


def expand_spatial(weight, bias, band, groups, one, two):
    half = 0.5 * column_of(bias[...], CH, lambda i, l: i == l)
    parts = pieces(half)
    taps = weight.shape[1]
    depth = (taps + 1) * CH
    spread = (iota((taps, depth), 1) // CH == iota((taps, depth), 0)).astype(BF16)
    wide = jnp.dot(weight[...] * jnp.bfloat16(0.5), spread, preferred_element_type=F32)
    col = iota((CH, depth), 1)
    bias_row = jnp.where(
        col == taps * CH,
        parts[0],
        jnp.where(col == taps * CH + 1, parts[1], jnp.where(col == taps * CH + 2, parts[2], 0.0)),
    )
    in_taps = col < taps * CH
    slot = col & (CH - 1)

    def block(wanted):
        return jnp.where(in_taps, jnp.where(slot == wanted, wide, 0.0), bias_row)

    for b in range(CH):
        one[b * CH : (b + 1) * CH, :] = block(b).astype(BF16)
    slots = [0, 1, 2, 3, 4, 5, 8, 9, 10, 12, 13, 14]
    for n, s in enumerate(slots):
        value = block(s)
        if 8 <= s < 12:
            value = jnp.where(band > 0, value, 0.0)
        if s >= 12:
            value = jnp.where(band < groups - 1, value, 0.0)
        two[n * CH : (n + 1) * CH, :] = value.astype(BF16)


def expand_spectral(weight, bias, out):
    depth = out.shape[1]
    rows = 24
    half = 0.5 * column_of(bias[...], CH, lambda i, l: i == l)
    parts = pieces(half)
    spread = ((iota((CH, depth), 1) & (CH - 1)) == iota((CH, depth), 0)).astype(BF16)
    wide = jnp.dot(weight[...] * jnp.bfloat16(0.5), spread, preferred_element_type=F32)
    col = iota((rows, depth), 1)
    slot = col >> 4
    place = jnp.where(slot < BANDS, slot + HALO, jnp.where(slot < BANDS + HALO, slot - BANDS, slot))
    band = iota((rows, depth), 0)
    tap = jnp.where((slot < SLOTS) & (band < BANDS), place - band, -1)
    taps = weight.shape[0] // CH
    for k in range(CH):
        block = jnp.where(col == ACT, parts[0][k : k + 1], 0.0)
        block = jnp.where(col == ACT + 1, parts[1][k : k + 1], block)
        block = jnp.where(col == ACT + 2, parts[2][k : k + 1], block)
        for d in range(taps):
            block = jnp.where(tap == d, wide[d * CH + k : d * CH + k + 1], block)
        out[k * rows : (k + 1) * rows, :] = block.astype(BF16)


def slot_vectors(smalls):
    own, below, above = (s[...] for s in smalls)

    def column(n):
        return (
            column_of(own[n : n + 1], 32, lambda i, l: (i == l) & (i < BANDS))
            + column_of(below[n : n + 1], 32, lambda i, l: (i - 24 + BANDS - HALO == l) & (i >= 24) & (i < 24 + HALO))
            + column_of(above[n : n + 1], 32, lambda i, l: (i - 28 == l) & (i >= 28) & (i < 28 + HALO))
        )

    shift = column(0).astype(jnp.int32)
    step = jnp.broadcast_to(column(1), (32, LANES))
    lane = iota((32, LANES), 1)
    within = jnp.broadcast_to(shift & (LANES - 1), (32, LANES))
    index = (lane + within) & (LANES - 1)
    steps = (shift >> 7) + jnp.where(lane + within >= LANES, 1, 0)
    return index, steps, step


def refresh(cube, aperture, edges, residual, vectors, inside, upd):
    width = cube.shape[1]
    index, steps, step = vectors
    is0, is1, is2 = steps == 0, steps == 1, steps == 2
    margin = jnp.zeros((32, LANES), BF16)
    upd[:, 0:LANES] = margin
    upd[:, LANES + width : 2 * LANES + width] = margin

    def pull(t):
        at = pl.ds(pl.multiple_of(t * LANES, LANES), LANES)
        return gather_lanes(jnp.broadcast_to(residual[:, at], (32, LANES)), index)

    def tile(t, carry):
        p0, p1, p2 = carry
        p3 = pull(t + 3)
        at = pl.ds(pl.multiple_of(t * LANES, LANES), LANES)
        pulled = jnp.where(is0, p0, jnp.where(is1, p1, jnp.where(is2, p2, p3)))
        cubes = jnp.concatenate(
            [
                cube[:, at].astype(F32),
                jnp.zeros((2, LANES), F32),
                edges[0, :, at].astype(F32),
                edges[1, :, at].astype(F32),
            ]
        )
        new = cubes + pulled * aperture[:, at].astype(F32) * step
        if inside is not None:
            new = jnp.where(inside, new, 0.0)
        upd[:, pl.ds(pl.multiple_of(t * LANES + LANES, LANES), LANES)] = new.astype(BF16)
        return p1, p2, p3

    lax.fori_loop(0, width // LANES, tile, (pull(0), pull(1), pull(2)), unroll=4)


def denoise(upd, one, two, spectral, out_weight, actives, out):
    width = out.shape[1]
    count = width // TILE
    ones = jnp.ones((CH, TILE), BF16)
    for active in actives:
        active[ACT:, :] = ones
    project_out = column_of(out_weight[...], CH, lambda i, l: i == l)

    def spatial(t, active):
        start = pl.multiple_of(t * TILE, TILE)
        window = [upd[i, :, pl.ds(start, TILE + 2 * LANES)] for i in range(3)]
        shifted = [window[i][:, LANES - 1 + j : LANES - 1 + j + TILE] for i in range(3) for j in range(3)]
        for weight, group, at in ((one, slice(0, 16), 0), (two, slice(16, 32), 16 * CH)):
            patch = jnp.concatenate([s[group] for s in shifted] + [ones])
            half = jnp.dot(weight[...], patch, preferred_element_type=F32)
            active[at : at + half.shape[0], :] = (half * jnp.tanh(half) + half).astype(BF16)

    def rest(t, active):
        start = pl.multiple_of(t * TILE, TILE)
        half = jnp.dot(spectral[...], active[...], preferred_element_type=F32)
        total = upd[1, 0:24, pl.ds(pl.multiple_of(start + LANES, LANES), TILE)].astype(F32)
        for k in range(CH):
            h = half[k * 24 : (k + 1) * 24]
            total = total + project_out[k : k + 1] * (h * jnp.tanh(h) + h)
        out[:, pl.ds(start, TILE)] = total[0:BANDS].astype(BF16)

    first, second = actives
    spatial(0, first)

    def pair(p, carry):
        spatial(2 * p + 1, second)
        rest(2 * p, first)
        spatial(2 * p + 2, first)
        rest(2 * p + 1, second)
        return carry

    lax.fori_loop(0, count // 2 - 1, pair, 0)
    spatial(count - 1, second)
    rest(count - 2, first)
    rest(count - 1, second)


def whole_kernel(
    sizes,
    cube, aperture, meas, shears, steps, sw, sb, pw, pb, ow, out,
    part, low, high, small, parts, smalls, cube_up, cube_down, ap_up, ap_down, edges, res, res_up, res_down, counts,
    one, two, spectral, upd, act_a, act_b, send, recv,
):
    groups, nrow, ncol = sizes
    band, row, col = lax.axis_index("band"), lax.axis_index("row"), lax.axis_index("col")
    last = nrow * ncol - 1
    flat = row * ncol + col
    not_first, not_last = flat > 0, flat < last

    def device(db, dr):
        r = jnp.clip(flat + dr, 0, last)
        return (lax.rem(band + db + groups, groups), r // ncol, lax.rem(r, ncol))

    barrier = pltpu.get_barrier_semaphore()

    def greet(db, dr):
        pl.semaphore_signal(barrier, inc=1, device_id=device(db, dr), device_id_type=MESH)

    for db in (1, 2, -1):
        greet(db, 0)

    @pl.when(not_first)
    def _():
        greet(0, -1)

    @pl.when(not_last)
    def _():
        greet(0, 1)

    pack_small(shears, steps, small)
    pack_edges(cube, low, high)
    project(cube, aperture, shears, part)

    pl.semaphore_wait(barrier, 3 + not_first.astype(jnp.int32) + not_last.astype(jnp.int32))
    used = [0]

    def copy(src, dst, peer):
        n = used[0]
        used[0] += 1
        return pltpu.make_async_remote_copy(
            src_ref=src, dst_ref=dst, send_sem=send.at[n], recv_sem=recv.at[n],
            device_id=device(*peer), device_id_type=MESH,
        )

    down, up = (0, 1), (0, -1)
    tiny = [copy(small, smalls.at[n], (db, 0)) for n, db in enumerate((1, -1, 2))]
    partial = [copy(part, parts.at[n], (db, 0)) for n, db in enumerate((1, -1, 2))]
    edge = [copy(high, edges.at[1, 0], (1, 0)), copy(low, edges.at[1, 1], (-1, 0))]
    to_down = [copy(aperture, ap_up, down), copy(cube, cube_up, down)]
    to_up = [copy(aperture, ap_down, up), copy(cube, cube_down, up)]
    relay_down, relay_up = copy(edges.at[1], edges.at[0], down), copy(edges.at[1], edges.at[2], up)
    res_to_down, res_to_up = copy(res, res_up, down), copy(res, res_down, up)

    for c in tiny + partial + edge:
        c.start()

    @pl.when(not_last)
    def _():
        for c in to_down:
            c.start()

    @pl.when(not_first)
    def _():
        for c in to_up:
            c.start()

    expand_spatial(sw, sb, band, groups, one, two)
    expand_spectral(pw, pb, spectral)
    for c in edge:
        c.wait_recv()

    @pl.when(not_last)
    def _():
        relay_down.start()

    @pl.when(not_first)
    def _():
        relay_up.start()

    for c in tiny:
        c.wait_recv()
    count_open(aperture, [small, smalls.at[0], smalls.at[1], smalls.at[2]], counts)
    for c in partial:
        c.wait_recv()
    width = meas.shape[1]
    predicted = part[...] + (parts[0] + parts[1] + parts[2])
    tail = width // LANES * LANES
    res[:, tail:] = jnp.zeros((1, res.shape[1] - tail), F32)
    res[:, 0:width] = (meas[...] - predicted[:, 0:width]) / jnp.maximum(counts[:, 0:width], 1.0)

    @pl.when(not_last)
    def _():
        res_to_down.start()

    @pl.when(not_first)
    def _():
        res_to_up.start()

    vectors = slot_vectors((small, smalls.at[0], smalls.at[1]))
    refresh(cube, aperture, edges.at[1], res, vectors, None, upd.at[1])

    @pl.when(not_first)
    def _():
        for c in to_down + [relay_down, res_to_down]:
            c.wait_recv()
        refresh(cube_up, ap_up, edges.at[0], res_up, vectors, None, upd.at[0])

    @pl.when(jnp.logical_not(not_first))
    def _():
        upd[0] = jnp.zeros(upd.shape[1:], BF16)

    @pl.when(not_last)
    def _():
        for c in to_up + [relay_up, res_to_up]:
            c.wait_recv()
        refresh(cube_down, ap_down, edges.at[2], res_down, vectors, None, upd.at[2])

    @pl.when(jnp.logical_not(not_last))
    def _():
        upd[2] = jnp.zeros(upd.shape[1:], BF16)

    denoise(upd, one, two, spectral, ow, (act_a, act_b), out)
    for c in tiny + partial + edge:
        c.wait_send()

    @pl.when(not_last)
    def _():
        for c in to_down + [relay_down, res_to_down]:
            c.wait_send()

    @pl.when(not_first)
    def _():
        for c in to_up + [relay_up, res_to_up]:
            c.wait_send()


def solution(mesh):
    sizes = tuple(mesh.shape[a] for a in ("band", "row", "col"))
    vmem = pl.BlockSpec(memory_space=pltpu.VMEM)

    def on_device(cube, aperture, meas, shears, steps, sw, sb, pw, pb, ow):
        width = cube.shape[2]
        cube = cube.reshape(cube.shape[0], width)
        shears, steps, sb, pb, ow = (a.reshape(1, -1) for a in (shears, steps, sb, pb, ow))
        pw = pw.reshape(-1, CH)
        wide = (meas.shape[1] + 2 * LANES - 1) // LANES * LANES
        line = pltpu.VMEM((1, wide), F32)
        out = pl.pallas_call(
            lambda *r: whole_kernel(sizes, *r),
            name="whole",
            out_shape=jax.ShapeDtypeStruct(cube.shape, BF16),
            in_specs=[vmem] * 10,
            out_specs=vmem,
            scratch_shapes=[
                line,
                pltpu.VMEM((4, width), BF16),
                pltpu.VMEM((4, width), BF16),
                pltpu.VMEM((8, LANES), F32),
                pltpu.VMEM((3, 1, wide), F32),
                pltpu.VMEM((3, 8, LANES), F32),
                pltpu.VMEM(cube.shape, BF16),
                pltpu.VMEM(cube.shape, BF16),
                pltpu.VMEM(aperture.shape, jnp.int32),
                pltpu.VMEM(aperture.shape, jnp.int32),
                pltpu.VMEM((3, 2, 4, width), BF16),
                line,
                line,
                line,
                line,
                pltpu.VMEM((16 * CH, 10 * CH), BF16),
                pltpu.VMEM((12 * CH, 10 * CH), BF16),
                pltpu.VMEM((24 * CH, ACT + CH), BF16),
                pltpu.VMEM((3, 32, width + 2 * LANES), BF16),
                pltpu.VMEM((ACT + CH, TILE), BF16),
                pltpu.VMEM((ACT + CH, TILE), BF16),
                pltpu.SemaphoreType.DMA((16,)),
                pltpu.SemaphoreType.DMA((16,)),
            ],
            compiler_params=pltpu.CompilerParams(collective_id=0, has_side_effects=True),
        )(cube, aperture, meas, shears, steps, sw, sb, pw, pb, ow)
        return out.reshape(out.shape[0], 1, width)

    in_specs = (
        P("band", ("row", "col"), None),
        P(("row", "col"), None),
        P(("row", "col"), None),
        P("band"),
        P("band"),
        P(),
        P(),
        P(),
        P(),
        P(),
    )
    return jax.shard_map(
        on_device, mesh=mesh, in_specs=in_specs, out_specs=P("band", ("row", "col"), None), check_vma=False
    )
```

time: 54.4 us -> 31.6 us (0.58)
  the two profiles are of different devices: /device:TPU:16 before, /device:TPU:448 now
where the time goes in v2:
time: 31.6 us; the launch traced here: 31.5 us
  Pallas kernels  29.8 us (94%)
  local copies, waits for them, and re-layouts  1.62 us (5%)
    pallas_call x1, Pallas kernels, on_device(): pl.pallas_call(lambda *r: whole_kernel(sizes, *r), name='whole', out_shap...  29.8 us
    unnamed x1, local copies, waits for them, and re-layouts  1.62 us

profile of v2, /device:TPU:448, one launch (start us, length us, event | category | flops | bytes accessed | tf_op | source)
XLA Modules:
  0.0 31.5 jit_solution(6206520785239848231)
XLA Ops:
  0.0 29.8 %whole.1 = bf16[22,4096]{1,0:T(8,128)(2,1)} custom-call(bf16[22,4096]{1,0:T(8,128)(2,1)} %bitcast.9, s32[1,4096]{1,0:T(1,128)} %r_1_.1, f32[1,4444]{1,0:T(1,128)} %r_2_.1, s32[1,22]{1,0:T(1,128)} %bitcast.11, f32[1,22]{1,0:T(1,128)} %bitcast.12, bf16[16,9]{1,0:T(8,128)(2,1)} %r_5_.1, f32[1,16]{1,0:T(1,128)} %bitcast.13, bf16[112,16]{1,0:T(8,128)(2,1)} %bitcast.10, ...), custom_call_target="tpu_custom_call" | custom-call | tf_op jit(solution)/shard_map/whole/pallas_call | solution.py:396
  29.8 1.6 %copy.12 = bf16[22,1,4096]{2,0,1:T(8,128)(2,1)} copy(bf16[22,1,4096]{2,0,1:T(8,128)(2,1)} %bitcast.8) | data formatting | bytes 360448

commit v3 on v2

--- a/solution.py
+++ b/solution.py
@@ -38,46 +38,45 @@
     return jnp.take_along_axis(x, index, axis=1, mode="promise_in_bounds")
 
 
-def place(tiles, shift, out, tile_of):
-    rows = shift.shape[0]
-    lane = iota((rows, LANES), 1)
-    within = jnp.broadcast_to(shift & (LANES - 1), (rows, LANES))
+def place(tiles, row, acc, tile_of, add):
+    shift = column_of(row, 24, lambda i, l: i == l).astype(jnp.int32)
+    lane = iota((24, LANES), 1)
+    within = jnp.broadcast_to(shift & (LANES - 1), (24, LANES))
     index = (lane - within) & (LANES - 1)
     steps = (shift >> 7) + jnp.where(lane < within, 1, 0)
     is0, is1, is2 = steps == 0, steps == 1, steps == 2
-    none = jnp.zeros((rows, LANES), F32)
+    none = jnp.zeros((24, LANES), F32)
     turned = []
-    for t in range(out.shape[1] // LANES):
+    for t in range(acc.shape[1] // LANES):
+        at = slice(t * LANES, (t + 1) * LANES)
         turned.append(gather_lanes(tile_of(t), index) if t < tiles else none)
         back = [turned[t - e] if t >= e else none for e in range(4)]
         here = jnp.where(is0, back[0], jnp.where(is1, back[1], jnp.where(is2, back[2], back[3])))
-        out[:, t * LANES : (t + 1) * LANES] = jnp.sum(here, axis=0, keepdims=True)
-
-
-def shift_column(row):
-    return column_of(row, 24, lambda i, l: i == l).astype(jnp.int32)
-
-
-def project(cube, aperture, shears, part):
+        total = here[0:8] + here[8:16] + here[16:24]
+        acc[:, at] = acc[:, at] + total if add else total
+
+
+def collapse(acc, out):
+    out[...] = jnp.sum(acc[...], axis=0, keepdims=True)
+
+
+def project(cube, aperture, shears, acc):
     def masked(t):
         at = slice(t * LANES, (t + 1) * LANES)
         bands = jnp.concatenate([cube[:, at].astype(F32), jnp.zeros((24 - BANDS, LANES), F32)])
         return bands * aperture[:, at].astype(F32)
 
-    place(cube.shape[1] // LANES, shift_column(shears[...].astype(F32)), part, masked)
-
-
-def count_open(aperture, smalls, out):
-    shift = jnp.concatenate([shift_column(s[0:1]) for s in smalls])
-    shape = (shift.shape[0], LANES)
-    group_row = jnp.concatenate([iota((24, LANES), 0)] * len(smalls))
-    own = group_row < BANDS
+    place(cube.shape[1] // LANES, shears[...].astype(F32), acc, masked, False)
+
+
+def count_open(aperture, small, acc, add):
+    own = iota((24, LANES), 0) < BANDS
 
     def opened(t):
         open_t = aperture[:, t * LANES : (t + 1) * LANES].astype(F32)
-        return jnp.where(own, jnp.broadcast_to(open_t, shape), 0.0)
-
-    place(aperture.shape[1] // LANES, shift, out, opened)
+        return jnp.where(own, jnp.broadcast_to(open_t, (24, LANES)), 0.0)
+
+    place(aperture.shape[1] // LANES, small[0:1], acc, opened, add)
 
 
 def pack_small(shears, steps, small):
@@ -128,21 +127,19 @@
 
 def expand_spectral(weight, bias, out):
     depth = out.shape[1]
-    rows = 24
+    rows = 8
     half = 0.5 * column_of(bias[...], CH, lambda i, l: i == l)
     parts = pieces(half)
     spread = ((iota((CH, depth), 1) & (CH - 1)) == iota((CH, depth), 0)).astype(BF16)
     wide = jnp.dot(weight[...] * jnp.bfloat16(0.5), spread, preferred_element_type=F32)
     col = iota((rows, depth), 1)
-    slot = col >> 4
-    place = jnp.where(slot < BANDS, slot + HALO, jnp.where(slot < BANDS + HALO, slot - BANDS, slot))
-    band = iota((rows, depth), 0)
-    tap = jnp.where((slot < SLOTS) & (band < BANDS), place - band, -1)
+    start = depth - CH
+    tap = jnp.where(col < start, (col >> 4) - iota((rows, depth), 0), -1)
     taps = weight.shape[0] // CH
     for k in range(CH):
-        block = jnp.where(col == ACT, parts[0][k : k + 1], 0.0)
-        block = jnp.where(col == ACT + 1, parts[1][k : k + 1], block)
-        block = jnp.where(col == ACT + 2, parts[2][k : k + 1], block)
+        block = jnp.where(col == start, parts[0][k : k + 1], 0.0)
+        block = jnp.where(col == start + 1, parts[1][k : k + 1], block)
+        block = jnp.where(col == start + 2, parts[2][k : k + 1], block)
         for d in range(taps):
             block = jnp.where(tap == d, wide[d * CH + k : d * CH + k + 1], block)
         out[k * rows : (k + 1) * rows, :] = block.astype(BF16)
@@ -167,20 +164,21 @@
     return index, steps, step
 
 
-def refresh(cube, aperture, edges, residual, vectors, inside, upd):
+def refresh(cube, aperture, edges, residual, vectors, upd):
     width = cube.shape[1]
+    tiles = width // LANES
     index, steps, step = vectors
     is0, is1, is2 = steps == 0, steps == 1, steps == 2
-    margin = jnp.zeros((32, LANES), BF16)
-    upd[:, 0:LANES] = margin
-    upd[:, LANES + width : 2 * LANES + width] = margin
+    lane = iota((32, LANES), 1)
+    leftmost, rightmost = lane == 0, lane == LANES - 1
+    none = jnp.zeros((32, LANES), F32)
 
     def pull(t):
         at = pl.ds(pl.multiple_of(t * LANES, LANES), LANES)
         return gather_lanes(jnp.broadcast_to(residual[:, at], (32, LANES)), index)
 
     def tile(t, carry):
-        p0, p1, p2 = carry
+        p0, p1, p2, before, after = carry
         p3 = pull(t + 3)
         at = pl.ds(pl.multiple_of(t * LANES, LANES), LANES)
         pulled = jnp.where(is0, p0, jnp.where(is1, p1, jnp.where(is2, p2, p3)))
@@ -193,61 +191,70 @@
             ]
         )
         new = cubes + pulled * aperture[:, at].astype(F32) * step
-        if inside is not None:
-            new = jnp.where(inside, new, 0.0)
-        upd[:, pl.ds(pl.multiple_of(t * LANES + LANES, LANES), LANES)] = new.astype(BF16)
-        return p1, p2, p3
-
-    lax.fori_loop(0, width // LANES, tile, (pull(0), pull(1), pull(2)), unroll=4)
-
-
-def denoise(upd, one, two, spectral, out_weight, actives, out):
+        up, down = pltpu.roll(new, 1, 1), pltpu.roll(new, LANES - 1, 1)
+        upd[0, :, at] = jnp.where(leftmost, before, up).astype(BF16)
+        upd[1, :, at] = new.astype(BF16)
+        upd[2, :, at] = jnp.where(rightmost, down, after).astype(BF16)
+        return p1, p2, p3, up, down
+
+    last = lax.fori_loop(0, tiles, tile, (pull(0), pull(1), pull(2), none, none), unroll=4)
+    upd[2, :, tiles * LANES : (tiles + 1) * LANES] = jnp.where(rightmost, 0.0, last[4]).astype(BF16)
+
+
+def denoise(upd, one, two, spectral, out_weight, active, out):
     width = out.shape[1]
     count = width // TILE
     ones = jnp.ones((CH, TILE), BF16)
-    for active in actives:
-        active[ACT:, :] = ones
-    project_out = column_of(out_weight[...], CH, lambda i, l: i == l)
-
-    def spatial(t, active):
+    active[ACT:, :] = jnp.zeros((active.shape[0] - ACT, TILE), BF16)
+    weights = column_of(out_weight[...], CH, lambda i, l: i == l)
+    own = HALO * CH
+
+    def spatial(t):
         start = pl.multiple_of(t * TILE, TILE)
-        window = [upd[i, :, pl.ds(start, TILE + 2 * LANES)] for i in range(3)]
-        shifted = [window[i][:, LANES - 1 + j : LANES - 1 + j + TILE] for i in range(3) for j in range(3)]
-        for weight, group, at in ((one, slice(0, 16), 0), (two, slice(16, 32), 16 * CH)):
+        shifted = [upd[i, j, :, pl.ds(pl.multiple_of(start + j // 2 * LANES, LANES), TILE)] for i in range(3) for j in range(3)]
+        halves = []
+        for weight, group in ((one, slice(0, 16)), (two, slice(16, 32))):
             patch = jnp.concatenate([s[group] for s in shifted] + [ones])
             half = jnp.dot(weight[...], patch, preferred_element_type=F32)
-            active[at : at + half.shape[0], :] = (half * jnp.tanh(half) + half).astype(BF16)
-
-    def rest(t, active):
+            halves.append((half * jnp.tanh(half) + half).astype(BF16))
+        first, second = halves
+        top = own + first.shape[0]
+        edge = second.shape[0] - 2 * own
+        active[own:top, :] = first
+        active[top : top + edge, :] = second[0:edge]
+        active[0:own, :] = second[edge : edge + own]
+        active[top + edge : ACT, :] = second[edge + own :]
+
+    def rest(t):
         start = pl.multiple_of(t * TILE, TILE)
-        half = jnp.dot(spectral[...], active[...], preferred_element_type=F32)
-        total = upd[1, 0:24, pl.ds(pl.multiple_of(start + LANES, LANES), TILE)].astype(F32)
-        for k in range(CH):
-            h = half[k * 24 : (k + 1) * 24]
-            total = total + project_out[k : k + 1] * (h * jnp.tanh(h) + h)
-        out[:, pl.ds(start, TILE)] = total[0:BANDS].astype(BF16)
-
-    first, second = actives
-    spatial(0, first)
-
-    def pair(p, carry):
-        spatial(2 * p + 1, second)
-        rest(2 * p, first)
-        spatial(2 * p + 2, first)
-        rest(2 * p + 1, second)
+        centre = upd[1, 1, 0:24, pl.ds(start, TILE)].astype(F32)
+        totals = []
+        for g in range(3):
+            source = jnp.concatenate([active[g * 8 * CH : (g * 8 + 14) * CH, :], ones])
+            half = jnp.dot(spectral[...], source, preferred_element_type=F32)
+            total = centre[g * 8 : (g + 1) * 8]
+            for k in range(CH):
+                h = half[k * 8 : (k + 1) * 8]
+                total = total + weights[k : k + 1] * (h * jnp.tanh(h) + h)
+            totals.append(total)
+        out[:, pl.ds(start, TILE)] = jnp.concatenate(totals)[0:BANDS].astype(BF16)
+
+    spatial(0)
+
+    def body(t, carry):
+        rest(t)
+        spatial(t + 1)
         return carry
 
-    lax.fori_loop(0, count // 2 - 1, pair, 0)
-    spatial(count - 1, second)
-    rest(count - 2, first)
-    rest(count - 1, second)
+    lax.fori_loop(0, count - 1, body, 0)
+    rest(count - 1)
 
 
 def whole_kernel(
     sizes,
     cube, aperture, meas, shears, steps, sw, sb, pw, pb, ow, out,
-    part, low, high, small, parts, smalls, cube_up, cube_down, ap_up, ap_down, edges, res, res_up, res_down, counts,
-    one, two, spectral, upd, act_a, act_b, send, recv,
+    part, low, high, small, parts, smalls, cube_up, cube_down, ap_up, ap_down, edges, res, res_up, res_down, acc, counts,
+    one, two, spectral, upd, active, send, recv,
 ):
     groups, nrow, ncol = sizes
     band, row, col = lax.axis_index("band"), lax.axis_index("row"), lax.axis_index("col")
@@ -277,8 +284,6 @@
 
     pack_small(shears, steps, small)
     pack_edges(cube, low, high)
-    project(cube, aperture, shears, part)
-
     pl.semaphore_wait(barrier, 3 + not_first.astype(jnp.int32) + not_last.astype(jnp.int32))
     used = [0]
 
@@ -299,7 +304,11 @@
     relay_down, relay_up = copy(edges.at[1], edges.at[0], down), copy(edges.at[1], edges.at[2], up)
     res_to_down, res_to_up = copy(res, res_up, down), copy(res, res_down, up)
 
-    for c in tiny + partial + edge:
+    for c in tiny + edge:
+        c.start()
+    project(cube, aperture, shears, acc)
+    collapse(acc, part)
+    for c in partial:
         c.start()
 
     @pl.when(not_last)
@@ -312,7 +321,6 @@
         for c in to_up:
             c.start()
 
-    expand_spatial(sw, sb, band, groups, one, two)
     expand_spectral(pw, pb, spectral)
     for c in edge:
         c.wait_recv()
@@ -325,9 +333,13 @@
     def _():
         relay_up.start()
 
+    expand_spatial(sw, sb, band, groups, one, two)
+    count_open(aperture, small, acc, False)
     for c in tiny:
         c.wait_recv()
-    count_open(aperture, [small, smalls.at[0], smalls.at[1], smalls.at[2]], counts)
+    for n in range(3):
+        count_open(aperture, smalls.at[n], acc, True)
+    collapse(acc, counts)
     for c in partial:
         c.wait_recv()
     width = meas.shape[1]
@@ -345,13 +357,13 @@
         res_to_up.start()
 
     vectors = slot_vectors((small, smalls.at[0], smalls.at[1]))
-    refresh(cube, aperture, edges.at[1], res, vectors, None, upd.at[1])
+    refresh(cube, aperture, edges.at[1], res, vectors, upd.at[1])
 
     @pl.when(not_first)
     def _():
         for c in to_down + [relay_down, res_to_down]:
             c.wait_recv()
-        refresh(cube_up, ap_up, edges.at[0], res_up, vectors, None, upd.at[0])
+        refresh(cube_up, ap_up, edges.at[0], res_up, vectors, upd.at[0])
 
     @pl.when(jnp.logical_not(not_first))
     def _():
@@ -361,13 +373,13 @@
     def _():
         for c in to_up + [relay_up, res_to_up]:
             c.wait_recv()
-        refresh(cube_down, ap_down, edges.at[2], res_down, vectors, None, upd.at[2])
+        refresh(cube_down, ap_down, edges.at[2], res_down, vectors, upd.at[2])
 
     @pl.when(jnp.logical_not(not_last))
     def _():
         upd[2] = jnp.zeros(upd.shape[1:], BF16)
 
-    denoise(upd, one, two, spectral, ow, (act_a, act_b), out)
+    denoise(upd, one, two, spectral, ow, active, out)
     for c in tiny + partial + edge:
         c.wait_send()
 
@@ -414,13 +426,13 @@
                 line,
                 line,
                 line,
+                pltpu.VMEM((8, wide), F32),
                 line,
                 pltpu.VMEM((16 * CH, 10 * CH), BF16),
                 pltpu.VMEM((12 * CH, 10 * CH), BF16),
-                pltpu.VMEM((24 * CH, ACT + CH), BF16),
-                pltpu.VMEM((3, 32, width + 2 * LANES), BF16),
-                pltpu.VMEM((ACT + CH, TILE), BF16),
-                pltpu.VMEM((ACT + CH, TILE), BF16),
+                pltpu.VMEM((8 * CH, 15 * CH), BF16),
+                pltpu.VMEM((3, 3, 32, width + LANES), BF16),
+                pltpu.VMEM((ACT + 2 * CH, TILE), BF16),
                 pltpu.SemaphoreType.DMA((16,)),
                 pltpu.SemaphoreType.DMA((16,)),
             ],

time: 31.6 us -> 31.2 us (0.987)
  Pallas kernels: 29.8 us -> 29.4 us
    pallas_call x1, Pallas kernels: 29.8 us -> 29.4 us  [on_device(): pl.pallas_call(lambda *r: whole_kernel(sizes, *r), name='whole', out_shap...]
where the time goes in v3:
time: 31.2 us; the launch traced here: 31.1 us
  Pallas kernels  29.4 us (94%)
  local copies, waits for them, and re-layouts  1.62 us (5%)
    pallas_call x1, Pallas kernels, on_device(): pl.pallas_call(lambda *r: whole_kernel(sizes, *r), name='whole', out_shap...  29.4 us
    unnamed x1, local copies, waits for them, and re-layouts  1.62 us

profile of v3, /device:TPU:448, one launch (start us, length us, event | category | flops | bytes accessed | tf_op | source)
XLA Modules:
  0.0 31.1 jit_solution(17932078599934931841)
XLA Ops:
  0.0 29.4 %whole.1 = bf16[22,4096]{1,0:T(8,128)(2,1)} custom-call(bf16[22,4096]{1,0:T(8,128)(2,1)} %bitcast.9, s32[1,4096]{1,0:T(1,128)} %r_1_.1, f32[1,4444]{1,0:T(1,128)} %r_2_.1, s32[1,22]{1,0:T(1,128)} %bitcast.11, f32[1,22]{1,0:T(1,128)} %bitcast.12, bf16[16,9]{1,0:T(8,128)(2,1)} %r_5_.1, f32[1,16]{1,0:T(1,128)} %bitcast.13, bf16[112,16]{1,0:T(8,128)(2,1)} %bitcast.10, ...), custom_call_target="tpu_custom_call" | custom-call | tf_op jit(solution)/shard_map/whole/pallas_call | solution.py:408
  29.4 1.6 %copy.12 = bf16[22,1,4096]{2,0,1:T(8,128)(2,1)} copy(bf16[22,1,4096]{2,0,1:T(8,128)(2,1)} %bitcast.8) | data formatting | bytes 360448

commit v4 on v3

--- a/solution.py
+++ b/solution.py
@@ -436,7 +436,7 @@
                 pltpu.SemaphoreType.DMA((16,)),
                 pltpu.SemaphoreType.DMA((16,)),
             ],
-            compiler_params=pltpu.CompilerParams(collective_id=0, has_side_effects=True),
+            compiler_params=pltpu.CompilerParams(collective_id=0, has_side_effects=True, vmem_limit_bytes=16 * 2**20),
         )(cube, aperture, meas, shears, steps, sw, sb, pw, pb, ow)
         return out.reshape(out.shape[0], 1, width)
 

time: 31.2 us -> 32.6 us (1.045)
  local copies, waits for them, and re-layouts: 1.62 us -> 4.49 us
  Pallas kernels: 29.4 us -> 27.8 us
    unnamed x1 -> x21, local copies, waits for them, and re-layouts: 1.62 us -> 4.49 us
    pallas_call x1, Pallas kernels: 29.4 us -> 27.8 us  [on_device(): pl.pallas_call(lambda *r: whole_kernel(sizes, *r), name='whole', out_shap...]
where the time goes in v4:
time: 32.6 us; the launch traced here: 32.3 us
  Pallas kernels  27.8 us (85%)
  local copies, waits for them, and re-layouts  4.49 us (14%)
    pallas_call x1, Pallas kernels, on_device(): pl.pallas_call(lambda *r: whole_kernel(sizes, *r), name='whole', out_shap...  27.8 us
    unnamed x21, local copies, waits for them, and re-layouts  4.49 us

profile of v4, /device:TPU:448, one launch (start us, length us, event | category | flops | bytes accessed | tf_op | source)
XLA Modules:
  0.0 32.3 jit_solution(11012535459144832771)
XLA Ops:
  0.0 0.0 copy-start.4
  0.0 0.0 copy-start.8
  0.0 0.0 copy-start.9
  0.0 0.0 copy-start.5
  0.0 0.0 copy-start.6
  0.0 0.0 copy-start.7
  0.0 0.6 %copy-done.4 = bf16[16,9]{1,0:T(8,128)(2,1)S(1)} copy-done((bf16[16,9]{1,0:T(8,128)(2,1)S(1)}, bf16[16,9]{1,0:T(8,128)(2,1)}, u32[]{:S(2)}) %copy-start.4) | copy-done | bytes 312
  0.7 0.0 copy-done.8
  0.7 0.0 copy-done.9
  0.7 0.0 copy-done.5
  0.7 0.0 copy-done.6
  0.7 0.0 copy-done.7
  0.7 0.0 copy-start
  0.7 0.9 %copy-done = bf16[22,1,4096]{2,0,1:T(8,128)(2,1)S(1)} copy-done((bf16[22,1,4096]{2,0,1:T(8,128)(2,1)S(1)}, bf16[22,1,4096]{2,0,1:T(8,128)(2,1)}, u32[]{:S(2)}) %copy-start) | copy-done | bytes 180248
  1.7 0.0 copy-start.1
  1.7 0.7 %copy-done.1 = bf16[7,16,16]{2,1,0:T(8,128)(2,1)S(1)} copy-done((bf16[7,16,16]{2,1,0:T(8,128)(2,1)S(1)}, bf16[7,16,16]{2,1,0:T(8,128)(2,1)}, u32[]{:S(2)}) %copy-start.1) | copy-done | bytes 3608
  2.4 0.0 copy-start.2
  2.4 0.7 %copy-done.2 = f32[1,4444]{1,0:T(1,128)S(1)} copy-done((f32[1,4444]{1,0:T(1,128)S(1)}, f32[1,4444]{1,0:T(1,128)}, u32[]{:S(2)}) %copy-start.2) | copy-done | bytes 17800
  3.1 0.0 copy-start.3
  3.1 0.7 %copy-done.3 = s32[1,4096]{1,0:T(1,128)S(1)} copy-done((s32[1,4096]{1,0:T(1,128)S(1)}, s32[1,4096]{1,0:T(1,128)}, u32[]{:S(2)}) %copy-start.3) | copy-done | bytes 16408
  3.9 27.8 %whole.1 = bf16[22,4096]{1,0:T(8,128)(2,1)S(1)} custom-call(bf16[22,4096]{1,0:T(8,128)(2,1)S(1)} %bitcast.9, s32[1,4096]{1,0:T(1,128)S(1)} %copy-done.3, f32[1,4444]{1,0:T(1,128)S(1)} %copy-done.2, s32[1,22]{1,0:T(1,128)S(1)} %bitcast.11, f32[1,22]{1,0:T(1,128)S(1)} %bitcast.12, bf16[16,9]{1,0:T(8,128)(2,1)S(1)} %copy-done.4, f32[1,16]{1,0:T(1,128)S(1)} %bitcast.13, ...), custom_call_target="tpu_custom_call" | custom-call | tf_op jit(solution)/shard_map/whole/pallas_call | solution.py:408
  31.6 0.7 %copy.12 = bf16[22,1,4096]{2,0,1:T(8,128)(2,1)} copy(bf16[22,1,4096]{2,0,1:T(8,128)(2,1)S(1)} %bitcast.8) | data formatting | bytes 360448
Async XLA Ops:
  0.0 0.7 %copy-start.4 = (bf16[16,9]{1,0:T(8,128)(2,1)S(1)}, bf16[16,9]{1,0:T(8,128)(2,1)}, u32[]{:S(2)}) copy-start(bf16[16,9]{1,0:T(8,128)(2,1)} %r_5_.1) | copy-start | bytes 868
  0.0 0.7 %copy-start.8 = (f32[16]{0:T(128)S(1)}, f32[16]{0:T(128)}, u32[]{:S(2)}) copy-start(f32[16]{0:T(128)} %param.18) | copy-start | bytes 196
  0.0 0.7 %copy-start.9 = (f32[16]{0:T(128)S(1)}, f32[16]{0:T(128)}, u32[]{:S(2)}) copy-start(f32[16]{0:T(128)} %param.19) | copy-start | bytes 196
  0.0 0.7 %copy-start.5 = (s32[22]{0:T(128)S(1)}, s32[22]{0:T(128)}, u32[]{:S(2)}) copy-start(s32[22]{0:T(128)} %param.13) | copy-start | bytes 268
  0.0 0.7 %copy-start.6 = (f32[22]{0:T(128)S(1)}, f32[22]{0:T(128)}, u32[]{:S(2)}) copy-start(f32[22]{0:T(128)} %param.14) | copy-start | bytes 268
  0.0 0.7 %copy-start.7 = (f32[16]{0:T(128)S(1)}, f32[16]{0:T(128)}, u32[]{:S(2)}) copy-start(f32[16]{0:T(128)} %param.16) | copy-start | bytes 196
  0.7 0.9 %copy-start = (bf16[22,1,4096]{2,0,1:T(8,128)(2,1)S(1)}, bf16[22,1,4096]{2,0,1:T(8,128)(2,1)}, u32[]{:S(2)}) copy-start(bf16[22,1,4096]{2,0,1:T(8,128)(2,1)} %param.10) | copy-start | bytes 540676
  1.7 0.7 %copy-start.1 = (bf16[7,16,16]{2,1,0:T(8,128)(2,1)S(1)}, bf16[7,16,16]{2,1,0:T(8,128)(2,1)}, u32[]{:S(2)}) copy-start(bf16[7,16,16]{2,1,0:T(8,128)(2,1)} %param.17) | copy-start | bytes 10756
  2.4 0.7 %copy-start.2 = (f32[1,4444]{1,0:T(1,128)S(1)}, f32[1,4444]{1,0:T(1,128)}, u32[]{:S(2)}) copy-start(f32[1,4444]{1,0:T(1,128)} %r_2_.1) | copy-start | bytes 53332
  3.1 0.7 %copy-start.3 = (s32[1,4096]{1,0:T(1,128)S(1)}, s32[1,4096]{1,0:T(1,128)}, u32[]{:S(2)}) copy-start(s32[1,4096]{1,0:T(1,128)} %r_1_.1) | copy-start | bytes 49156
